TPU v7x, 128 devices: a whole 4x4x4 slice. The times are simulated.
128 devices in a mesh: seq: 8 (over z, core), exp: 16 (over x, y).
Axes of the slice: x: 4, y: 4, z: 4, core: 2. Of those that a mesh axis runs over, the one named last changes fastest.
Arguments:
- residual: bfloat16 [16384, 8192], P(('seq', 'exp')), may hold values from -6 to 6
- expert_rows: bfloat16 [8, 16, 16, 24, 8192], P('seq', 'exp'), may hold values from -6 to 6
- expert_ids: int32 [16384, 2], P(('seq', 'exp')), may hold values from 0 to 15, as said below
- expert_slots: int32 [16384, 2], P(('seq', 'exp')), may hold values from 0 to 23, as said below
- combine_weights: float32 [16384, 2], P(('seq', 'exp')), may hold values from 0.1 to 0.9
- norm_gain: float32 [8192], replicated, may hold values from 0.1 to 1.9
- in_weight: bfloat16 [8192, 8192], P(None, 'exp'), may hold values from -0.0625 to 0.0625
- conv_weight: float32 [4, 8192], P(None, 'exp'), may hold values from -3 to 3
- conv_bias: float32 [8192], P('exp'), may hold values from -0.5 to 0.5
- bc_weight: bfloat16 [8192, 128], P('exp'), may hold values from -0.00390625 to 0.00390625
- dt_weight: bfloat16 [8192, 128], P('exp'), may hold values from -0.0625 to 0.0625
- dt_bias: float32 [128], P('exp'), may hold values from -2 to 0.5
- decay_log: float32 [128], P('exp'), may hold values from -14 to -3.2
- skip_gain: float32 [128], P('exp'), may hold values from -1 to 3
Outputs:
- scan_output: bfloat16 [16384, 8192], P('seq', 'exp')
Inputs may be any that keep to these rules, and one draw needn't show every extreme that they name: `expert_ids`: A token's two ids differ. The tokens of one device name no expert more than 24 times, and in each span one expert is named exactly 24 times by the tokens of every device of the span. `expert_slots`: A token's slot at its k-th expert counts the earlier (token, k) pairs of the same device, in row-major order, that name the same expert.
All inputs are finite; a program needn't handle non-finite values.
Results may differ from a plain program's by a relative error of at most 0.0074.
Values may be sent and summed in bfloat16 or wider, within the bound.
No kernel may reach another device: no remote copies, remote signals or barrier semaphores. Data moves between devices by JAX's collectives and lax.ppermute only.
A program may use at most 320 MiB of HBM per device.

v0:
```python
import jax
import jax.numpy as jnp
from jax import lax
from jax.sharding import PartitionSpec as P

TOPK = 2
KCONV = 4
HEAD = 64
NSTATE = 64
STRETCH = 256


def passed_along(value, axis, steps):
    count = lax.axis_size(axis)
    leading, last = (max(0, -steps), min(count, count - steps))
    return lax.ppermute(value, axis, [(source, source + steps) for source in range(leading, last)])


def block_terms(b_rows, c_rows, steps_dt, decays, values):
    running = jnp.cumsum(decays, axis=0)
    scores = jnp.dot(c_rows, b_rows.T, preferred_element_type=jnp.float32)
    length = running.shape[0]
    causal = (jnp.arange(length)[:, None] >= jnp.arange(length)[None, :])[:, :, None]
    decay_gap = jnp.where(causal, running[:, None, :] - running[None, :, :], 0.0)
    mixing = jnp.where(
        causal, jnp.exp(decay_gap) * scores[:, :, None] * steps_dt[None, :, :], 0.0
    ).astype(jnp.bfloat16)
    inside = jnp.einsum("tsh,shp->thp", mixing, values, preferred_element_type=jnp.float32)
    carried = jnp.exp(running[-1][None, :] - running) * steps_dt
    states = jnp.einsum(
        "sn,shp->hnp",
        b_rows.astype(jnp.float32),
        carried[:, :, None] * values.astype(jnp.float32),
        precision=lax.Precision.HIGHEST,
    )
    return (running, inside, states, jnp.exp(running[-1]))


def shards(
    residual,
    expert_rows,
    expert_ids,
    expert_slots,
    combine_weights,
    norm_gain,
    in_weight,
    conv_weight,
    conv_bias,
    bc_weight,
    dt_weight,
    dt_bias,
    decay_log,
    skip_gain,
):
    own_rows, width = residual.shape
    returned = lax.all_to_all(expert_rows, "exp", split_axis=2, concat_axis=1, tiled=True)
    capacity = returned.shape[3]
    buffers = returned.reshape(returned.shape[1] * capacity, width)
    picked = jnp.take(buffers, expert_ids * capacity + expert_slots, axis=0)
    mixture = jnp.zeros((own_rows, width), jnp.float32)
    for column in range(TOPK):
        mixture = mixture + combine_weights[:, column][:, None] * picked[:, column].astype(
            jnp.float32
        )
    stream = residual.astype(jnp.float32) + mixture
    factor = lax.rsqrt(jnp.mean(stream * stream, axis=1, keepdims=True) + 1e-06)
    normed = (stream * factor * norm_gain[None, :]).astype(jnp.bfloat16)
    group_rows = own_rows * lax.axis_size("exp")
    local_width = in_weight.shape[1]
    x_in = jnp.dot(
        lax.all_gather(normed, "exp", axis=0, tiled=True),
        in_weight,
        preferred_element_type=jnp.float32,
    ).astype(jnp.bfloat16)
    rim_rows = passed_along(x_in[group_rows - (KCONV - 1) :], "seq", 1)
    padded = jnp.concatenate([rim_rows, x_in], axis=0)
    filtered = jnp.zeros((group_rows, local_width), jnp.float32) + conv_bias[None, :]
    for tap in range(KCONV):
        filtered = filtered + conv_weight[tap][None, :] * padded[tap : tap + group_rows].astype(
            jnp.float32
        )
    activated = jax.nn.silu(filtered).astype(jnp.bfloat16)
    state_part = jnp.dot(activated, bc_weight, preferred_element_type=jnp.float32)
    rate_part = jnp.dot(activated, dt_weight, preferred_element_type=jnp.float32)
    state_proj, dt_raw = lax.psum((state_part, rate_part), "exp")
    heads_here = local_width // HEAD
    first_head = lax.axis_index("exp") * heads_here
    steps_dt = jax.nn.softplus(
        lax.dynamic_slice_in_dim(dt_raw, first_head, heads_here, 1) + dt_bias[None, :]
    )
    decays = -jnp.exp(decay_log)[None, :] * steps_dt
    b_all = state_proj[:, :NSTATE].astype(jnp.bfloat16)
    c_all = state_proj[:, NSTATE:].astype(jnp.bfloat16)
    blocks = group_rows // STRETCH
    c_blocks = c_all.reshape(blocks, STRETCH, NSTATE)
    value_blocks = activated.reshape(blocks, STRETCH, heads_here, HEAD)

    def advance(carry, inputs):
        local_states, prefix_decay = carry
        b_rows, c_rows, block_dt, block_decays, values = inputs
        running, inside, states, total = block_terms(b_rows, c_rows, block_dt, block_decays, values)
        return (
            (total[:, None, None] * local_states + states, prefix_decay * total),
            (running, inside, local_states, prefix_decay),
        )

    start_carry = (
        jnp.zeros((heads_here, NSTATE, HEAD), jnp.float32),
        jnp.ones((heads_here,), jnp.float32),
    )
    (final_states, device_decay), (runnings, insides, starts, prefixes) = lax.scan(
        advance,
        start_carry,
        (
            b_all.reshape(blocks, STRETCH, NSTATE),
            c_blocks,
            steps_dt.reshape(blocks, STRETCH, heads_here),
            decays.reshape(blocks, STRETCH, heads_here),
            value_blocks,
        ),
    )
    empty_states = jnp.zeros((heads_here, NSTATE, HEAD), jnp.float32)

    def relay_turn(turn, carried):
        incoming, outgoing = carried
        incoming = passed_along(outgoing, "seq", 1)
        return (incoming, device_decay[:, None, None] * incoming + final_states)

    incoming, outgoing_last = lax.fori_loop(
        0, lax.axis_size("seq") - 1, relay_turn, (empty_states, final_states)
    )
    entering = starts + prefixes[:, :, None, None] * incoming[None]
    across = jnp.exp(runnings)[:, :, :, None] * jnp.einsum(
        "btn,bhnp->bthp", c_blocks.astype(jnp.float32), entering, precision=lax.Precision.HIGHEST
    )
    output = insides + across + skip_gain[None, None, :, None] * value_blocks.astype(jnp.float32)
    return output.astype(jnp.bfloat16).reshape(group_rows, local_width)


def solution(mesh):
    placed = (
        P(("seq", "exp"), None),
        P("seq", "exp", None, None, None),
        P(("seq", "exp"), None),
        P(("seq", "exp"), None),
        P(("seq", "exp"), None),
        P(),
        P(None, "exp"),
        P(None, "exp"),
        P("exp"),
        P("exp", None),
        P("exp", None),
        P("exp"),
        P("exp"),
        P("exp"),
    )
    return jax.shard_map(
        shards, mesh=mesh, in_specs=placed, out_specs=P("seq", "exp"), check_vma=False
    )
```

profile of v0, /device:TPU:1, one launch (start us, length us, event | category | flops | bytes accessed | tf_op | source)
XLA Modules:
  0.0 613.9 jit_solution(3130771036729045118)
XLA Ops:
  6.5 7.8 %all-to-all-start = ((bf16[1,1,16,24,8192]{4,3,1,0,2:T(8,128)(2,1)}), bf16[1,1,16,24,8192]{4,3,1,0,2:T(8,128)(2,1)}, u32[]{:S(2)}, u32[]{:S(2)}) async-start(bf16[1,1,16,24,8192]{4,3,1,0,2:T(8,128)(2,1)} %bitcast.113), calls=%async_computation | async-start | bytes 12582912 | tf_op jit(solution)/shard_map/all_to_all | solution.py:56
  14.7 100.4 %all-to-all-done = bf16[1,1,16,24,8192]{4,3,1,0,2:T(8,128)(2,1)} async-done(((bf16[1,1,16,24,8192]{4,3,1,0,2:T(8,128)(2,1)}), bf16[1,1,16,24,8192]{4,3,1,0,2:T(8,128)(2,1)}, u32[]{:S(2)}, u32[]{:S(2)}) %all-to-all-start) | async-done | bytes 6291488 | tf_op jit(solution)/shard_map/all_to_all | solution.py:56
  115.1 12.6 %gather_fusion = bf16[256,8192]{1,0:T(8,128)(2,1)} fusion(bf16[384,8192]{1,0:T(8,128)(2,1)} %bitcast.3, s32[1024]{0:T(1024)S(1)} %pad_clamp_fusion), kind=kCustom, calls=%fused_computation | custom fusion | bytes 8389632 | tf_op jit(solution)/shard_map/jit(_take)/gather | solution.py:59
  127.7 7.6 %reshape.94 = bf16[128,2,8192]{2,1,0:T(2,128)(2,1)} reshape(bf16[256,8192]{1,0:T(8,128)(2,1)} %gather_fusion) | data formatting | bytes 8388608 | tf_op jit(solution)/shard_map/jit(_take)/gather | solution.py:59
  135.3 7.2 %copy_select_fusion = bf16[128,2,8192]{2,0,1:T(8,128)(2,1)S(1)} fusion(bf16[128,2,8192]{2,1,0:T(2,128)(2,1)} %reshape.94, pred[128,2]{0,1:T(4,128)(4,1)S(1)} %get-tuple-element.250), kind=kLoop, calls=%fused_computation.47 | loop fusion | flops 2097152 | bytes 8388864 | tf_op jit(solution)/shard_map/jit(_take)/select_n | solution.py:59
  142.6 1.4 multiply_reduce_fusion
  144.0 3.0 multiply_convert_fusion.1
  147.1 205.3 %all-gather.2.cloned.1.call-done = bf16[2048,8192]{1,0:T(8,128)(2,1)} async-done(((bf16[128,8192]{1,0:T(8,128)(2,1)}), bf16[2048,8192]{1,0:T(8,128)(2,1)}) %all-gather.2.cloned.1.call-update) | async-done | bytes 33554448 | tf_op jit(solution)/shard_map/all_gather | solution.py:71
  352.4 23.7 %convolution_convert_fusion = bf16[2048,512]{1,0:T(8,128)(2,1)S(1)} fusion(bf16[2048,8192]{1,0:T(8,128)(2,1)} %all-gather.2.cloned.1.call-done, bf16[8192,512]{1,0:T(8,128)(2,1)} %param.24), kind=kOutput, calls=%fused_computation.52 | convolution fusion | flops 17180917760 | bytes 44040192 | tf_op jit(solution)/shard_map/dot_general | solution.py:70
  376.2 1.3 copy-done.4
  377.5 3.7 collective-permute-start.1
  382.0 6.0 multiply_convert_fusion
  388.0 1.8 fusion.34
  389.8 1.7 fusion.35
  391.5 3.6 reshape.109
  395.2 4.0 copy.57
  399.2 75.3 %all-reduce.4 = bf16[2048,128]{1,0:T(8,128)(2,1)S(1)} all-reduce(f32[2048,128]{1,0:T(8,128)} %fusion.35), channel_id=1, replica_groups=mesh['seq'=8,'exp'=16] {'exp'}, use_global_device_ids=true, to_apply=%region_1.2 | all-reduce | flops 262144 | bytes 1572864 | tf_op jit(solution)/shard_map/psum | solution.py:85
  475.5 1.2 copy.58
  477.9 38.5 %while.34 = (s32[]{:T(128)}, f32[8,64,64]{1,2,0:T(8,128)S(1)}, f32[8]{0:T(128)S(1)}, f32[8,256,8]{1,2,0:T(8,128)}, f32[8,256,8,64]{1,3,2,0:T(8,128)}, /*index=5*...) while((s32[]{:T(128)}, f32[8,64,64]{1,2,0:T(8,128)S(1)}, ...), condition=%wide.region_6.7_spmd.clone, body=%wide.region_3.6_spmd.clone.sunk | while | flops 180033568 | bytes 2758157 | solution.py:111
  479.3 1.6 fusion.62
  484.1 1.6 fusion.62
  488.9 1.6 fusion.62
  493.7 1.6 fusion.62
  498.5 1.6 fusion.62
  503.3 1.6 fusion.62
  508.1 1.6 fusion.62
  513.0 1.5 fusion.62
  516.6 71.0 %while.33 = (s32[]{:T(128)}, f32[8,64,64]{2,1,0:T(8,128)}, f32[8,64,64]{2,1,0:T(8,128)S(1)}, f32[8]{0:T(128)S(1)}, f32[8,64,64]{2,1,0:T(8,128)S(1)}, /*index=5*/s32[]{:T(128)}) while((s32[]{:T(128)}, f32[8,64,64]{2,1,0:T(8,128)}, f32[8,64,64]{2,1,0:T(8,128)S(1)}, f32[8]{0:T(128)S(1)}, f32[8,64,64]{2,1,0:T(8,128)S(1)}, ...), condition=%wide.region_8.9_spmd, body=%wide.region_7.8_spmd.sunk | while | flops 65538 | bytes 1441961 | solution.py:129
  516.6 16.7 %collective-permute-start = (f32[8,64,64]{2,1,0:T(8,128)S(1)}, f32[8,64,64]{2,1,0:T(8,128)S(1)}, u32[]{:S(2)}, u32[]{:S(2)}) collective-permute-start(f32[8,64,64]{2,1,0:T(8,128)S(1)} %get-tuple-element.428), channel_id=1, source_target_pairs={{0,16},{16,32},{32,48},{48,64},{64,80},{80,96},{96,112},{1,17},{17... | collective-permute-start | bytes 393224 | tf_op jit(solution)/shard_map/while/body/eval_jaxpr/ppermute | solution.py:16
  533.3 3.3 collective-permute-done
  537.3 4.4 collective-permute-start
  541.7 3.3 collective-permute-done
  545.7 4.4 collective-permute-start
  550.1 3.3 collective-permute-done
  554.1 4.4 collective-permute-start
  558.5 3.3 collective-permute-done
  562.5 4.4 collective-permute-start
  566.8 3.3 collective-permute-done
  570.8 4.4 collective-permute-start
  575.2 3.3 collective-permute-done
  579.2 4.4 collective-permute-start
  583.6 3.3 collective-permute-done
  587.6 1.1 copy.61
  588.7 1.8 multiply_add_fusion.1
  590.5 1.8 fusion.36
  592.7 2.8 add_convert_fusion
  595.6 5.1 copy.67
  600.6 6.4 %reshape.108 = bf16[2048,512]{1,0:T(8,128)(2,1)} reshape(bf16[8,256,8,64]{3,2,1,0:T(8,128)(2,1)} %copy.67) | data formatting | bytes 4194304 | tf_op jit(solution)/shard_map/reshape | solution.py:137
  (197 shorter events, 34.4 us)
Async XLA Ops:
  6.5 381.5 %copy-start = (bf16[512,128]{1,0:T(8,128)(2,1)S(1)}, bf16[512,128]{1,0:T(8,128)(2,1)}, u32[]{:S(2)}) copy-start(bf16[512,128]{1,0:T(8,128)(2,1)} %param.28) | copy-start | bytes 393220
  6.5 7.8 %copy-start.10 = (s32[128,2]{0,1:T(2,128)S(1)}, s32[128,2]{0,1:T(2,128)}, u32[]{:S(2)}) copy-start(s32[128,2]{0,1:T(2,128)} %param.21) | copy-start | bytes 3076
  6.5 7.8 %copy-start.11 = (s32[128,2]{0,1:T(2,128)S(1)}, s32[128,2]{0,1:T(2,128)}, u32[]{:S(2)}) copy-start(s32[128,2]{0,1:T(2,128)} %param.20) | copy-start | bytes 3076
  6.5 8.1 %copy-start.12 = (f32[128,2]{0,1:T(2,128)S(1)}, f32[128,2]{0,1:T(2,128)}, u32[]{:S(2)}) copy-start(f32[128,2]{0,1:T(2,128)} %param.22) | copy-start | bytes 3076
  6.5 108.6 %all-to-all-start = ((bf16[1,1,16,24,8192]{4,3,1,0,2:T(8,128)(2,1)}), bf16[1,1,16,24,8192]{4,3,1,0,2:T(8,128)(2,1)}, u32[]{:S(2)}, u32[]{:S(2)}) async-start(bf16[1,1,16,24,8192]{4,3,1,0,2:T(8,128)(2,1)} %bitcast.113), calls=%async_computation | async-start | bytes 12582912 | tf_op jit(solution)/shard_map/all_to_all | solution.py:56
  14.3 338.1 %all-gather.2.cloned.1.call-start = ((), (), s32[]{:S(2)}) async-start(), calls=%async_computation.1 | async-start | bytes 35651584 | tf_op jit(solution)/shard_map/all_gather | solution.py:71
  135.3 7.2 %copy-start.2 = (bf16[128,8192]{1,0:T(8,128)(2,1)S(1)}, bf16[128,8192]{1,0:T(8,128)(2,1)}, u32[]{:S(2)}) copy-start(bf16[128,8192]{1,0:T(8,128)(2,1)} %param.18) | copy-start | bytes 6291460
  142.5 1.4 copy-start.7
  144.0 3.1 copy-start.8
  147.0 330.0 %all-reduce.3.cloned.1.call-start = ((), (), s32[]{:S(2)}) async-start(), calls=%async_computation.2 | async-start | bytes 2097152 | tf_op jit(solution)/shard_map/psum | solution.py:85
  147.1 234.2 %copy-start.15 = (f32[8]{0:T(128)S(1)}, f32[8]{0:T(128)}, u32[]{:S(2)}) copy-start(f32[8]{0:T(128)} %param.30) | copy-start | bytes 100
  147.1 234.9 %copy-start.9 = (f32[512]{0:T(512)S(1)}, f32[512]{0:T(512)}, u32[]{:S(2)}) copy-start(f32[512]{0:T(512)} %param.26) | copy-start | bytes 6148
  376.2 1.3 copy-start.4
  377.5 4.5 collective-permute-start.1
  382.0 7.8 %copy-start.5 = (bf16[512,128]{1,0:T(8,128)(2,1)S(1)}, bf16[512,128]{1,0:T(8,128)(2,1)}, u32[]{:S(2)}) copy-start(bf16[512,128]{1,0:T(8,128)(2,1)} %param.27) | copy-start | bytes 393220
  395.2 81.8 %copy-start.13 = (f32[8]{0:T(128)S(1)}, f32[8]{0:T(128)}, u32[]{:S(2)}) copy-start(f32[8]{0:T(128)} %param.29) | copy-start | bytes 100
  516.6 20.0 %collective-permute-start = (f32[8,64,64]{2,1,0:T(8,128)S(1)}, f32[8,64,64]{2,1,0:T(8,128)S(1)}, u32[]{:S(2)}, u32[]{:S(2)}) collective-permute-start(f32[8,64,64]{2,1,0:T(8,128)S(1)} %get-tuple-element.428), channel_id=1, source_target_pairs={{0,16},{16,32},{32,48},{48,64},{64,80},{80,96},{96,112},{1,17},{17... | collective-permute-start | bytes 393224 | tf_op jit(solution)/shard_map/while/body/eval_jaxpr/ppermute | solution.py:16
  536.6 0.7 copy-start.1
  537.3 7.7 %collective-permute-start = (f32[8,64,64]{2,1,0:T(8,128)S(1)}, f32[8,64,64]{2,1,0:T(8,128)S(1)}, u32[]{:S(2)}, u32[]{:S(2)}) collective-permute-start(f32[8,64,64]{2,1,0:T(8,128)S(1)} %get-tuple-element.428), channel_id=1, source_target_pairs={{0,16},{16,32},{32,48},{48,64},{64,80},{80,96},{96,112},{1,17},{17... | collective-permute-start | bytes 393224 | tf_op jit(solution)/shard_map/while/body/eval_jaxpr/ppermute | solution.py:16
  545.0 0.7 copy-start.1
  545.7 7.7 %collective-permute-start = (f32[8,64,64]{2,1,0:T(8,128)S(1)}, f32[8,64,64]{2,1,0:T(8,128)S(1)}, u32[]{:S(2)}, u32[]{:S(2)}) collective-permute-start(f32[8,64,64]{2,1,0:T(8,128)S(1)} %get-tuple-element.428), channel_id=1, source_target_pairs={{0,16},{16,32},{32,48},{48,64},{64,80},{80,96},{96,112},{1,17},{17... | collective-permute-start | bytes 393224 | tf_op jit(solution)/shard_map/while/body/eval_jaxpr/ppermute | solution.py:16
  553.4 0.7 copy-start.1
  554.1 7.7 %collective-permute-start = (f32[8,64,64]{2,1,0:T(8,128)S(1)}, f32[8,64,64]{2,1,0:T(8,128)S(1)}, u32[]{:S(2)}, u32[]{:S(2)}) collective-permute-start(f32[8,64,64]{2,1,0:T(8,128)S(1)} %get-tuple-element.428), channel_id=1, source_target_pairs={{0,16},{16,32},{32,48},{48,64},{64,80},{80,96},{96,112},{1,17},{17... | collective-permute-start | bytes 393224 | tf_op jit(solution)/shard_map/while/body/eval_jaxpr/ppermute | solution.py:16
  561.8 0.7 copy-start.1
  562.5 7.7 %collective-permute-start = (f32[8,64,64]{2,1,0:T(8,128)S(1)}, f32[8,64,64]{2,1,0:T(8,128)S(1)}, u32[]{:S(2)}, u32[]{:S(2)}) collective-permute-start(f32[8,64,64]{2,1,0:T(8,128)S(1)} %get-tuple-element.428), channel_id=1, source_target_pairs={{0,16},{16,32},{32,48},{48,64},{64,80},{80,96},{96,112},{1,17},{17... | collective-permute-start | bytes 393224 | tf_op jit(solution)/shard_map/while/body/eval_jaxpr/ppermute | solution.py:16
  570.1 0.7 copy-start.1
  570.8 7.7 %collective-permute-start = (f32[8,64,64]{2,1,0:T(8,128)S(1)}, f32[8,64,64]{2,1,0:T(8,128)S(1)}, u32[]{:S(2)}, u32[]{:S(2)}) collective-permute-start(f32[8,64,64]{2,1,0:T(8,128)S(1)} %get-tuple-element.428), channel_id=1, source_target_pairs={{0,16},{16,32},{32,48},{48,64},{64,80},{80,96},{96,112},{1,17},{17... | collective-permute-start | bytes 393224 | tf_op jit(solution)/shard_map/while/body/eval_jaxpr/ppermute | solution.py:16
  578.5 0.7 copy-start.1
  579.2 7.7 %collective-permute-start = (f32[8,64,64]{2,1,0:T(8,128)S(1)}, f32[8,64,64]{2,1,0:T(8,128)S(1)}, u32[]{:S(2)}, u32[]{:S(2)}) collective-permute-start(f32[8,64,64]{2,1,0:T(8,128)S(1)} %get-tuple-element.428), channel_id=1, source_target_pairs={{0,16},{16,32},{32,48},{48,64},{64,80},{80,96},{96,112},{1,17},{17... | collective-permute-start | bytes 393224 | tf_op jit(solution)/shard_map/while/body/eval_jaxpr/ppermute | solution.py:16
  586.9 0.7 copy-start.1
  590.5 1.9 copy-start.6
  590.5 2.2 copy-start.3
  590.5 2.2 copy-start.14
Sparse Core Ops, SparseCore 0:
  147.1 205.2 all-gather.1
  390.0 86.9 all-reduce.2
where the time goes:
time: 615 us; the launch traced here: 614 us
  waiting for transfers between devices  330 us (54%)
  blocking collectives  75.3 us (12%)
  starting transfers between devices  54.6 us (9%)
  local copies, waits for them, and re-layouts  52.2 us (8%)
  matrix products  46.7 us (8%)
  other arithmetic  41.4 us (7%)
  between operations  13.8 us (2%)
    all_gather x1, waiting for transfers between devices, shards(): lax.all_gather(normed, 'exp', axis=0, tiled=True)  205 us
    all_to_all x1, waiting for transfers between devices, shards(): lax.all_to_all(expert_rows, 'exp', split_axis=2, concat_axis=1, tiled=True)  100 us
    psum x1, blocking collectives, shards(): state_proj, dt_raw = lax.psum((state_part, rate_part), 'exp')  75.3 us
    ppermute x8, starting transfers between devices, passed_along(): lax.ppermute(value, axis, [(source, source + steps) for source in range(l...  46.7 us
    dot_general x1, matrix products, shards(): jnp.dot(lax.all_gather(normed, 'exp', axis=0, tiled=True), in_weight, pre...  23.7 us
    ppermute x8, waiting for transfers between devices, passed_along(): lax.ppermute(value, axis, [(source, source + steps) for source in range(l...  23.7 us
    gather x2, local copies, waits for them, and re-layouts, shards(): picked = jnp.take(buffers, expert_ids * capacity + expert_slots, axis=0)  20.2 us
    dot_general x8, matrix products, block_terms(): jnp.einsum('tsh,shp->thp', mixing, values, preferred_element_type=jnp.flo...  12.5 us
  transfers between devices with their start and end apart: 11, of which 11 were waited for; matrix products, arithmetic and copies ran while one was open for 2% of the time, Pallas kernels for 0%

commit v1 on v0

--- a/solution.py
+++ b/solution.py
@@ -68,7 +68,9 @@
     group_rows = own_rows * lax.axis_size("exp")
     local_width = in_weight.shape[1]
     x_in = jnp.dot(
-        lax.all_gather(normed, "exp", axis=0, tiled=True),
+        jnp.concatenate(
+            lax.all_to_all(jnp.stack([normed] * lax.axis_size("exp")), "exp", 0, 0), axis=0
+        ),
         in_weight,
         preferred_element_type=jnp.float32,
     ).astype(jnp.bfloat16)

time: 615 us -> 1050 us (1.71)
  waiting for transfers between devices: 330 us -> 741 us
  local copies, waits for them, and re-layouts: 52.2 us -> 63.1 us
    all_to_all x0 -> x1, waiting for transfers between devices: none -> 611 us  [shards(): lax.all_to_all(jnp.stack([normed] * lax.axis_size('exp')), 'exp', 0, 0)]
    all_gather x1 -> x0, waiting for transfers between devices: 205 us -> none  [shards(): lax.all_gather(normed, 'exp', axis=0, tiled=True)]
    all_to_all x0 -> x1, starting transfers between devices: none -> 11.5 us  [shards(): lax.all_to_all(jnp.stack([normed] * lax.axis_size('exp')), 'exp', 0, 0)]
    another operation x8 -> x9, local copies, waits for them, and re-layouts: 0.04 us -> 11 us  [the longest x1 11 us: shards(): jnp.stack([normed] * lax.axis_size('exp'))]
  transfers between devices with their start and end apart: 11 -> 11, of which waited for: 11 -> 11; matrix products, arithmetic and copies ran while one was open for 2% -> 1% of each run, Pallas kernels for 0% -> 0%
where the time goes in v1:
time: 1050 us; the launch traced here: 1040 us
  waiting for transfers between devices  741 us (71%)
  blocking collectives  75.4 us (7%)
  starting transfers between devices  64.2 us (6%)
  local copies, waits for them, and re-layouts  63.1 us (6%)
  matrix products  46.7 us (4%)
  other arithmetic  40.2 us (4%)
  between operations  13.8 us (1%)
    all_to_all x1, waiting for transfers between devices, shards(): lax.all_to_all(jnp.stack([normed] * lax.axis_size('exp')), 'exp', 0, 0)  611 us
    all_to_all x1, waiting for transfers between devices, shards(): lax.all_to_all(expert_rows, 'exp', split_axis=2, concat_axis=1, tiled=True)  100 us
    psum x1, blocking collectives, shards(): state_proj, dt_raw = lax.psum((state_part, rate_part), 'exp')  75.4 us
    ppermute x8, starting transfers between devices, passed_along(): lax.ppermute(value, axis, [(source, source + steps) for source in range(l...  44.9 us
    dot_general x1, matrix products, shards(): jnp.dot(jnp.concatenate(lax.all_to_all(jnp.stack([normed] * lax.axis_size...  23.8 us
    ppermute x8, waiting for transfers between devices, passed_along(): lax.ppermute(value, axis, [(source, source + steps) for source in range(l...  23.7 us
  transfers between devices with their start and end apart: 11, of which 11 were waited for; matrix products, arithmetic and copies ran while one was open for 1% of the time, Pallas kernels for 0%

profile of v1, /device:TPU:1, one launch (start us, length us, event | category | flops | bytes accessed | tf_op | source)
XLA Modules:
  0.0 1044.1 jit_solution(3027487828030560760)
XLA Ops:
  6.5 7.8 all-to-all-start
  14.6 100.5 %all-to-all-done = bf16[1,1,16,24,8192]{4,3,1,0,2:T(8,128)(2,1)} async-done(((bf16[1,1,16,24,8192]{4,3,1,0,2:T(8,128)(2,1)}), bf16[1,1,16,24,8192]{4,3,1,0,2:T(8,128)(2,1)}, u32[]{:S(2)}, u32[]{:S(2)}) %all-to-all-start) | async-done | bytes 6291488 | tf_op jit(solution)/shard_map/all_to_all | solution.py:56
  115.1 12.6 %gather_fusion = bf16[256,8192]{1,0:T(8,128)(2,1)} fusion(bf16[384,8192]{1,0:T(8,128)(2,1)} %bitcast.3, s32[1024]{0:T(1024)S(1)} %pad_clamp_fusion), kind=kCustom, calls=%fused_computation | custom fusion | bytes 8389632 | tf_op jit(solution)/shard_map/jit(_take)/gather | solution.py:59
  127.7 7.6 reshape.100
  135.3 7.2 copy_select_fusion
  142.5 1.4 multiply_reduce_fusion
  143.9 1.8 multiply_convert_fusion.1
  145.7 11.0 %stack.2 = bf16[16,128,8192]{2,1,0:T(8,128)(2,1)} broadcast(bf16[128,8192]{1,0:T(8,128)(2,1)S(1)} %multiply_convert_fusion.1), dimensions={1,2} | broadcast | bytes 35651584 | tf_op jit(solution)/shard_map/stack | solution.py:72
  156.7 11.5 %all-to-all-start.1 = ((bf16[16,128,8192]{2,1,0:T(8,128)(2,1)}), bf16[16,128,8192]{2,1,0:T(8,128)(2,1)}, u32[]{:S(2)}, u32[]{:S(2)}) async-start(bf16[16,128,8192]{2,1,0:T(8,128)(2,1)} %stack.2), calls=%async_computation.1 | async-start | bytes 67108864 | tf_op jit(solution)/shard_map/all_to_all | solution.py:72
  168.2 611.0 %all-to-all-done.1 = bf16[16,128,8192]{2,1,0:T(8,128)(2,1)} async-done(((bf16[16,128,8192]{2,1,0:T(8,128)(2,1)}), bf16[16,128,8192]{2,1,0:T(8,128)(2,1)}, u32[]{:S(2)}, u32[]{:S(2)}) %all-to-all-start.1) | async-done | bytes 33554464 | tf_op jit(solution)/shard_map/all_to_all | solution.py:72
  779.3 23.8 %convolution_convert_fusion = bf16[2048,512]{1,0:T(8,128)(2,1)S(1)} fusion(bf16[2048,8192]{1,0:T(8,128)(2,1)} %bitcast.7, bf16[8192,512]{1,0:T(8,128)(2,1)} %param.24), kind=kOutput, calls=%fused_computation.52 | convolution fusion | flops 17180917760 | bytes 44040192 | tf_op jit(solution)/shard_map/dot_general | solution.py:70
  804.4 6.5 collective-permute-start.1
  811.6 6.0 multiply_convert_fusion
  817.6 1.8 fusion.34
  819.5 1.7 fusion.35
  821.2 3.6 reshape.115
  824.8 4.0 copy.57
  828.8 75.4 %all-reduce.4 = bf16[2048,128]{1,0:T(8,128)(2,1)S(1)} all-reduce(f32[2048,128]{1,0:T(8,128)} %fusion.35), channel_id=1, replica_groups=mesh['seq'=8,'exp'=16] {'exp'}, use_global_device_ids=true, to_apply=%region_1.2 | all-reduce | flops 262144 | bytes 1572864 | tf_op jit(solution)/shard_map/psum | solution.py:87
  906.4 5.3 all-reduce.3.cloned.1.call-done
  912.7 38.5 %while.34 = (s32[]{:T(128)}, f32[8,64,64]{1,2,0:T(8,128)S(1)}, f32[8]{0:T(128)S(1)}, f32[8,256,8]{1,2,0:T(8,128)}, f32[8,256,8,64]{1,3,2,0:T(8,128)}, /*index=5*...) while((s32[]{:T(128)}, f32[8,64,64]{1,2,0:T(8,128)S(1)}, ...), condition=%wide.region_6.7_spmd.clone, body=%wide.region_3.6_spmd.clone.sunk | while | flops 180033568 | bytes 2758157 | solution.py:113
  914.0 1.6 fusion.62
  918.8 1.6 fusion.62
  923.6 1.6 fusion.62
  928.5 1.6 fusion.62
  933.3 1.6 fusion.62
  938.1 1.6 fusion.62
  942.9 1.6 fusion.62
  947.7 1.5 fusion.62
  951.4 66.4 %while.33 = (s32[]{:T(128)}, f32[8,64,64]{2,1,0:T(8,128)}, f32[8,64,64]{2,1,0:T(8,128)S(1)}, f32[8]{0:T(128)S(1)}, f32[8,64,64]{2,1,0:T(8,128)S(1)}, /*index=5*/s32[]{:T(128)}) while((s32[]{:T(128)}, f32[8,64,64]{2,1,0:T(8,128)}, f32[8,64,64]{2,1,0:T(8,128)S(1)}, f32[8]{0:T(128)S(1)}, f32[8,64,64]{2,1,0:T(8,128)S(1)}, ...), condition=%wide.region_8.9_spmd, body=%wide.region_7.8_spmd.sunk | while | flops 65538 | bytes 1441961 | solution.py:131
  951.4 12.2 %collective-permute-start = (f32[8,64,64]{2,1,0:T(8,128)S(1)}, f32[8,64,64]{2,1,0:T(8,128)S(1)}, u32[]{:S(2)}, u32[]{:S(2)}) collective-permute-start(f32[8,64,64]{2,1,0:T(8,128)S(1)} %get-tuple-element.428), channel_id=1, source_target_pairs={{0,16},{16,32},{32,48},{48,64},{64,80},{80,96},{96,112},{1,17},{17... | collective-permute-start | bytes 393224 | tf_op jit(solution)/shard_map/while/body/eval_jaxpr/ppermute | solution.py:16
  963.6 3.3 collective-permute-done
  967.6 4.4 collective-permute-start
  971.9 3.3 collective-permute-done
  975.9 4.4 collective-permute-start
  980.3 3.3 collective-permute-done
  984.3 4.4 collective-permute-start
  988.7 3.3 collective-permute-done
  992.7 4.4 collective-permute-start
  997.0 3.3 collective-permute-done
  1001.0 4.4 collective-permute-start
  1005.4 3.3 collective-permute-done
  1009.4 4.4 collective-permute-start
  1013.8 3.3 collective-permute-done
  1018.8 1.8 multiply_add_fusion.1
  1020.7 1.8 fusion.36
  1022.9 2.8 add_convert_fusion
  1025.7 5.1 copy.67
  1030.8 6.4 reshape.114
  (197 shorter events, 37.7 us)
Async XLA Ops:
  6.5 811.1 %copy-start = (bf16[512,128]{1,0:T(8,128)(2,1)S(1)}, bf16[512,128]{1,0:T(8,128)(2,1)}, u32[]{:S(2)}) copy-start(bf16[512,128]{1,0:T(8,128)(2,1)} %param.28) | copy-start | bytes 393220
  6.5 7.8 copy-start.10
  6.5 7.8 copy-start.11
  6.5 8.1 copy-start.12
  6.5 108.6 %all-to-all-start = ((bf16[1,1,16,24,8192]{4,3,1,0,2:T(8,128)(2,1)}), bf16[1,1,16,24,8192]{4,3,1,0,2:T(8,128)(2,1)}, u32[]{:S(2)}, u32[]{:S(2)}) async-start(bf16[1,1,16,24,8192]{4,3,1,0,2:T(8,128)(2,1)} %bitcast.114), calls=%async_computation | async-start | bytes 12582912 | tf_op jit(solution)/shard_map/all_to_all | solution.py:56
  135.3 7.2 copy-start.2
  142.5 1.4 copy-start.7
  156.7 11.5 %copy-start.8 = (f32[4,512]{1,0:T(4,128)S(1)}, f32[4,512]{1,0:T(4,128)}, u32[]{:S(2)}) copy-start(f32[4,512]{1,0:T(4,128)} %param.25) | copy-start | bytes 24580
  156.7 622.6 %all-to-all-start.1 = ((bf16[16,128,8192]{2,1,0:T(8,128)(2,1)}), bf16[16,128,8192]{2,1,0:T(8,128)(2,1)}, u32[]{:S(2)}, u32[]{:S(2)}) async-start(bf16[16,128,8192]{2,1,0:T(8,128)(2,1)} %stack.2), calls=%async_computation.1 | async-start | bytes 67108864 | tf_op jit(solution)/shard_map/all_to_all | solution.py:72
  168.2 743.5 %all-reduce.3.cloned.1.call-start = ((), (), s32[]{:S(2)}) async-start(), calls=%async_computation.2 | async-start | bytes 2097152 | tf_op jit(solution)/shard_map/psum | solution.py:87
  779.3 31.6 %copy-start.15 = (f32[8]{0:T(128)S(1)}, f32[8]{0:T(128)}, u32[]{:S(2)}) copy-start(f32[8]{0:T(128)} %param.30) | copy-start | bytes 100
  779.3 32.3 %copy-start.9 = (f32[512]{0:T(512)S(1)}, f32[512]{0:T(512)}, u32[]{:S(2)}) copy-start(f32[512]{0:T(512)} %param.26) | copy-start | bytes 6148
  803.1 1.3 copy-start.4
  804.4 7.2 collective-permute-start.1
  811.6 7.8 copy-start.5
  824.8 86.9 %copy-start.13 = (f32[8]{0:T(128)S(1)}, f32[8]{0:T(128)}, u32[]{:S(2)}) copy-start(f32[8]{0:T(128)} %param.29) | copy-start | bytes 100
  951.4 15.5 %collective-permute-start = (f32[8,64,64]{2,1,0:T(8,128)S(1)}, f32[8,64,64]{2,1,0:T(8,128)S(1)}, u32[]{:S(2)}, u32[]{:S(2)}) collective-permute-start(f32[8,64,64]{2,1,0:T(8,128)S(1)} %get-tuple-element.428), channel_id=1, source_target_pairs={{0,16},{16,32},{32,48},{48,64},{64,80},{80,96},{96,112},{1,17},{17... | collective-permute-start | bytes 393224 | tf_op jit(solution)/shard_map/while/body/eval_jaxpr/ppermute | solution.py:16
  966.9 0.7 copy-start.1
  967.6 7.7 collective-permute-start
  975.2 0.7 copy-start.1
  975.9 7.7 collective-permute-start
  983.6 0.7 copy-start.1
  984.3 7.7 collective-permute-start
  992.0 0.7 copy-start.1
  992.7 7.7 collective-permute-start
  1000.3 0.7 copy-start.1
  1001.0 7.7 collective-permute-start
  1008.7 0.7 copy-start.1
  1009.4 7.7 collective-permute-start
  1017.1 0.7 copy-start.1
  1020.7 1.9 copy-start.6
  1020.7 2.2 copy-start.3
  1020.7 2.2 copy-start.14
Sparse Core Ops, SparseCore 0:
  819.6 92.0 all-reduce.2
